TPU v7x, 256 devices: a whole 4x4x8 slice. The times are simulated.
256 devices in a mesh: seq: 64 (over y, z, x_hi), mp: 4 (over x_lo, core).
Axes of the slice: x: 4 (x_hi: 2, x_lo: 2; x = x_hi * 2 + x_lo), y: 4, z: 8, core: 2. Of those that a mesh axis runs over, the one named last changes fastest.
Arguments:
- stream: bfloat16 [20480, 1024], P('seq'), as said below
- gain_attn: float32 [1024], replicated, may hold values from 0.1 to 1.9
- gain_mlp: float32 [1024], replicated, may hold values from 0.1 to 1.9
- gain_read: float32 [1024], replicated, may hold values from 0.1 to 1.9
- query_weight: bfloat16 [1024, 1024], P(None, 'mp'), as said below
- key_weight: bfloat16 [1024, 1024], P(None, 'mp'), as said below
- value_weight: bfloat16 [1024, 1024], P(None, 'mp'), may hold values from -0.1875 to 0.1875
- out_weight: bfloat16 [1024, 1024], P('mp'), may hold values from -0.1875 to 0.1875
- up_weight: bfloat16 [1024, 2048], P(None, 'mp'), may hold values from -0.1875 to 0.1875
- down_weight: bfloat16 [2048, 1024], P('mp'), may hold values from -0.125 to 0.125
- read_weight: bfloat16 [1024, 8192], P(None, 'mp'), may hold values from -0.1875 to 0.1875
- read_bias: float32 [8192], P('mp'), may hold values from -3 to 3
- spike_counts: int32 [20480, 8192], P('seq', 'mp'), may hold values from 0 to 7
Outputs:
- log_rate: bfloat16 [20480, 8192], P('seq', 'mp')
- poisson_loss: float32 [20480], P('seq')
Inputs may be any that keep to these rules, and one draw needn't show every extreme that they name: Real-valued residual stream. `query_weight`: Real-valued projection. `key_weight`: Real-valued projection.
All inputs are finite; a program needn't handle non-finite values.
Results may differ from a plain program's by a relative error of at most 0.014.
Values may be sent and summed in bfloat16 or wider, within the bound.
A program may use at most 128 MiB of HBM per device.

v0:
```python
import jax
import jax.numpy as jnp
from jax import lax
from jax.sharding import PartitionSpec as P

DH = 64
NEU = 8192


def rms_norm(field, gain):
    wide = field.astype(jnp.float32)
    scale = lax.rsqrt(jnp.mean(wide * wide, axis=-1, keepdims=True) + 1e-05)
    return wide * scale * gain


def per_device(
    stream,
    gain_attn,
    gain_mlp,
    gain_read,
    query_weight,
    key_weight,
    value_weight,
    out_weight,
    up_weight,
    down_weight,
    read_weight,
    read_bias,
    spike_counts,
):
    shard_rows = stream.shape[0]
    my_index = lax.axis_index("seq")

    def position(device, within):
        return device * shard_rows + within

    normed = rms_norm(stream, gain_attn).astype(jnp.bfloat16)
    queries_flat = jnp.dot(normed, query_weight, preferred_element_type=jnp.float32).astype(
        jnp.bfloat16
    )
    keys_flat = jnp.dot(normed, key_weight, preferred_element_type=jnp.float32).astype(jnp.bfloat16)
    values_flat = jnp.dot(normed, value_weight, preferred_element_type=jnp.float32).astype(
        jnp.bfloat16
    )
    local_heads = queries_flat.shape[1] // DH
    factor = DH ** (-0.5)
    queries = queries_flat.reshape(shard_rows, local_heads, DH)
    query_pos = position(my_index, jnp.arange(shard_rows, dtype=jnp.int32))
    query_last = jnp.max(query_pos)
    init = (
        jnp.full((local_heads, shard_rows), -1e30, jnp.float32),
        jnp.zeros((local_heads, shard_rows), jnp.float32),
        jnp.zeros((local_heads, shard_rows, DH), jnp.float32),
    )
    state = init
    keys_piece = lax.all_gather(keys_flat, "seq", axis=0, tiled=True)
    values_piece = lax.all_gather(values_flat, "seq", axis=0, tiled=True)
    piece_rows = keys_piece.shape[0]
    gathered_rows = jnp.arange(piece_rows, dtype=jnp.int32)
    key_pos = position(gathered_rows // shard_rows, gathered_rows % shard_rows)
    block_rows = 512
    block_count = piece_rows // block_rows

    def one_block(inner_state, block_index):
        offset = block_index * block_rows
        key_block = lax.dynamic_slice_in_dim(keys_piece, offset, block_rows, 0).reshape(
            block_rows, local_heads, DH
        )
        value_block = lax.dynamic_slice_in_dim(values_piece, offset, block_rows, 0).reshape(
            block_rows, local_heads, DH
        )
        block_pos = lax.dynamic_slice_in_dim(key_pos, offset, block_rows, 0)

        def update(current):
            best, total_weight, accum = current
            scores = (
                jnp.einsum("qhd,khd->hqk", queries, key_block, preferred_element_type=jnp.float32)
                * factor
            )
            allowed = block_pos[None, None, :] <= query_pos[None, :, None]
            scores = jnp.where(allowed, scores, -1e30)
            fresh = jnp.maximum(best, jnp.max(scores, axis=-1))
            weights = jnp.where(allowed, jnp.exp(scores - fresh[..., None]), 0.0)
            decay = jnp.exp(best - fresh)
            total_weight = total_weight * decay + jnp.sum(weights, axis=-1)
            weights_low = weights.astype(jnp.bfloat16)
            accum = accum * decay[..., None] + jnp.einsum(
                "hqk,khd->hqd", weights_low, value_block, preferred_element_type=jnp.float32
            )
            return (fresh, total_weight, accum)

        def keep(current):
            return current

        return (lax.cond(jnp.min(block_pos) > query_last, keep, update, inner_state), None)

    state, unused = lax.scan(one_block, state, jnp.arange(block_count, dtype=jnp.int32))
    best, total_weight, accum = state
    attended = (
        jnp.transpose(accum / total_weight[..., None], (1, 0, 2))
        .reshape(shard_rows, local_heads * DH)
        .astype(jnp.bfloat16)
    )
    attn_part = jnp.dot(attended, out_weight, preferred_element_type=jnp.float32)
    attn_total = lax.psum(attn_part.astype(jnp.bfloat16), "mp").astype(jnp.float32)
    resid = (stream.astype(jnp.float32) + attn_total).astype(jnp.bfloat16)
    mlp_in = rms_norm(resid, gain_mlp).astype(jnp.bfloat16)
    hidden = jax.nn.gelu(
        jnp.dot(mlp_in, up_weight, preferred_element_type=jnp.float32), approximate=True
    ).astype(jnp.bfloat16)
    mlp_part = jnp.dot(hidden, down_weight, preferred_element_type=jnp.float32)
    outcome = resid.astype(jnp.float32) + lax.psum(mlp_part.astype(jnp.bfloat16), "mp").astype(
        jnp.float32
    )
    read_in = rms_norm(outcome, gain_read).astype(jnp.bfloat16)
    rate_full = jnp.dot(read_in, read_weight, preferred_element_type=jnp.float32) + read_bias
    loss_part = jnp.sum(jnp.exp(rate_full) - spike_counts.astype(jnp.float32) * rate_full, axis=-1)
    poisson_loss = lax.psum(loss_part, "mp") / NEU
    return (rate_full.astype(jnp.bfloat16), poisson_loss)


def solution(mesh):
    in_specs = (
        P("seq", None),
        P(),
        P(),
        P(),
        P(None, "mp"),
        P(None, "mp"),
        P(None, "mp"),
        P("mp", None),
        P(None, "mp"),
        P("mp", None),
        P(None, "mp"),
        P("mp"),
        P("seq", "mp"),
    )
    out_specs = (P("seq", "mp"), P("seq"))
    return jax.shard_map(
        per_device, mesh=mesh, in_specs=in_specs, out_specs=out_specs, check_vma=False
    )
```

profile of v0, /device:TPU:225, one launch (start us, length us, event | category | flops | bytes accessed | tf_op | source)
XLA Modules:
  0.0 770.5 jit_solution(6381487957085612974)
XLA Ops:
  7.3 1.5 fusion.14
  8.7 2.3 convolution_convert_fusion.4
  13.6 160.6 %all-gather.3.cloned.1.call-done = bf16[20480,256]{1,0:T(8,128)(2,1)} async-done(((bf16[320,256]{1,0:T(8,128)(2,1)}), bf16[20480,256]{1,0:T(8,128)(2,1)}) %all-gather.3.cloned.1.call-update) | async-done | bytes 10485776 | tf_op jit(solution)/shard_map/all_gather | solution.py:56
  174.2 14.2 %copy.19 = bf16[20480,256]{0,1:T(8,128)(2,1)} copy(bf16[20480,256]{1,0:T(8,128)(2,1)} %all-gather.3.cloned.1.call-done) | data formatting | bytes 20971520
  188.4 150.1 %all-gather.5.cloned.1.call-done = bf16[20480,256]{1,0:T(8,128)(2,1)} async-done(((bf16[320,256]{1,0:T(8,128)(2,1)}), bf16[20480,256]{1,0:T(8,128)(2,1)}) %all-gather.5.cloned.1.call-update) | async-done | bytes 10485776 | tf_op jit(solution)/shard_map/all_gather | solution.py:57
  338.5 14.2 %copy.20 = bf16[20480,256]{0,1:T(8,128)(2,1)} copy(bf16[20480,256]{1,0:T(8,128)(2,1)} %all-gather.5.cloned.1.call-done) | data formatting | bytes 20971520
  352.8 177.2 %while.15 = (s32[]{:T(128)}, f32[4,320]{1,0:T(4,128)S(1)}, f32[4,320]{1,0:T(4,128)S(1)}, f32[4,320,64]{1,2,0:T(8,128)S(1)}, s32[40]{0:T(128)S(1)}, /*index=5*/s3...) while((s32[]{:T(128)}, f32[4,320]{1,0:T(4,128)S(1)}, ...), condition=%wide.region_8.9_spmd.clone, body=%wide.region_2.8_spmd.clone.sunk | while | flops 176622912 | bytes 11005285 | solution.py:97
  356.1 4.3 conditional.3
  356.3 1.3 constant_dynamic-slice_fusion
  363.7 4.3 conditional.3
  363.9 1.3 constant_dynamic-slice_fusion
  371.4 4.3 conditional.3
  371.6 1.3 constant_dynamic-slice_fusion
  379.0 4.3 conditional.3
  379.2 1.3 constant_dynamic-slice_fusion
  386.7 4.3 conditional.3
  386.9 1.3 constant_dynamic-slice_fusion
  394.3 4.3 conditional.3
  394.5 1.3 constant_dynamic-slice_fusion
  402.0 4.3 conditional.3
  409.6 4.3 conditional.3
  417.3 4.3 conditional.3
  417.5 1.3 constant_dynamic-slice_fusion
  424.9 4.3 conditional.3
  425.1 1.3 constant_dynamic-slice_fusion
  531.4 170.2 %all-reduce.3.cloned.1.call-done = bf16[320,1024]{1,0:T(8,128)(2,1)} async-done(((bf16[320,1024]{1,0:T(8,128)(2,1)}), bf16[320,1024]{1,0:T(8,128)(2,1)}) %all-reduce.3.cloned.1.call-update) | async-done | bytes 655376 | tf_op jit(solution)/shard_map/psum | solution.py:105
  701.6 1.4 fusion.18
  703.0 3.1 convolution_convert_fusion
  706.2 44.4 %all-reduce.5.cloned.1.call-done = bf16[320,1024]{1,0:T(8,128)(2,1)} async-done(((bf16[320,1024]{1,0:T(8,128)(2,1)}), bf16[320,1024]{1,0:T(8,128)(2,1)}) %all-reduce.5.cloned.1.call-update) | async-done | bytes 655376 | tf_op jit(solution)/shard_map/psum | solution.py:112
  750.6 1.4 multiply_reduce_fusion
  752.1 6.2 subtract_reduce_fusion
  758.2 5.2 psum.23
  (333 shorter events, 90.7 us)
Async XLA Ops:
  7.2 695.8 %copy-start = (bf16[512,1024]{1,0:T(8,128)(2,1)S(1)}, bf16[512,1024]{1,0:T(8,128)(2,1)}, u32[]{:S(2)}) copy-start(bf16[512,1024]{1,0:T(8,128)(2,1)} %param.26) | copy-start | bytes 3145732
  7.2 4.0 copy-start.1
  7.2 4.0 copy-start.6
  7.2 4.0 copy-start.3
  7.2 5.1 copy-start.4
  7.2 167.0 %all-gather.3.cloned.1.call-start = ((), (), s32[]{:S(2)}) async-start(), calls=%async_computation | async-start | bytes 10649600 | tf_op jit(solution)/shard_map/all_gather | solution.py:56
  11.1 327.4 %all-gather.5.cloned.1.call-start = ((), (), s32[]{:S(2)}) async-start(), calls=%async_computation.1 | async-start | bytes 10649600 | tf_op jit(solution)/shard_map/all_gather | solution.py:57
  12.2 689.3 %all-reduce.3.cloned.1.call-start = ((), (), s32[]{:S(2)}) async-start(), calls=%async_computation.2 | async-start | bytes 1310720 | tf_op jit(solution)/shard_map/psum | solution.py:105
  352.8 177.3 %copy-start.2 = (bf16[256,1024]{1,0:T(8,128)(2,1)S(1)}, bf16[256,1024]{1,0:T(8,128)(2,1)}, u32[]{:S(2)}) copy-start(bf16[256,1024]{1,0:T(8,128)(2,1)} %param.24) | copy-start | bytes 1572868
  530.0 173.0 %copy-start.7 = (f32[1024]{0:T(1024)S(1)}, f32[1024]{0:T(1024)}, u32[]{:S(2)}) copy-start(f32[1024]{0:T(1024)} %param.19) | copy-start | bytes 12292
  531.3 219.3 %all-reduce.5.cloned.1.call-start = ((), (), s32[]{:S(2)}) async-start(), calls=%async_computation.3 | async-start | bytes 1310720 | tf_op jit(solution)/shard_map/psum | solution.py:112
  703.0 49.0 %copy-start.5 = (f32[2048]{0:T(1024)S(1)}, f32[2048]{0:T(1024)}, u32[]{:S(2)}) copy-start(f32[2048]{0:T(1024)} %param.28) | copy-start | bytes 24580
  703.0 49.0 %copy-start.8 = (f32[1024]{0:T(1024)S(1)}, f32[1024]{0:T(1024)}, u32[]{:S(2)}) copy-start(f32[1024]{0:T(1024)} %param.20) | copy-start | bytes 12292
Sparse Core Ops, SparseCore 0:
  12.1 162.0 all-gather.2
  177.7 160.7 all-gather.4
  531.4 170.0 all-reduce.2
  706.3 44.2 all-reduce.4
where the time goes:
time: 777 us; the launch traced here: 771 us
  waiting for transfers between devices  525 us (68%)
  loops' own time  81.2 us (10%)
  local copies, waits for them, and re-layouts  65.9 us (8%)
  other arithmetic  47.4 us (6%)
  matrix products  31.5 us (4%)
  between operations  14 us (2%)
    psum x1, waiting for transfers between devices, per_device(): lax.psum(attn_part.astype(jnp.bfloat16), 'mp').astype(jnp.float32)  170 us
    all_gather x1, waiting for transfers between devices, per_device(): keys_piece = lax.all_gather(keys_flat, 'seq', axis=0, tiled=True)  161 us
    all_gather x1, waiting for transfers between devices, per_device(): values_piece = lax.all_gather(values_flat, 'seq', axis=0, tiled=True)  150 us
    another operation x1, loops' own time, per_device(): lax.scan(one_block, state, jnp.arange(block_count, dtype=jnp.int32))  79.8 us
    psum x1, waiting for transfers between devices, per_device(): lax.psum(mlp_part.astype(jnp.bfloat16), 'mp').astype(jnp.float32)  44.4 us
    reduce_min x40, other arithmetic, one_block(): jnp.min(block_pos) > query_last  29.6 us
    unnamed x20, local copies, waits for them, and re-layouts  28.5 us
    dynamic_slice x40, local copies, waits for them, and re-layouts, per_device(): lax.scan(one_block, state, jnp.arange(block_count, dtype=jnp.int32))  23.5 us
  transfers between devices with their start and end apart: 4, of which 4 were waited for; matrix products, arithmetic and copies ran while one was open for 2% of the time, Pallas kernels for 0%

commit v1 on v0

v1 whole, which is shorter than its diff:
```python
import jax
import jax.numpy as jnp
from jax import lax
from jax.experimental import pallas as pl
from jax.experimental.pallas import tpu as pltpu
from jax.sharding import PartitionSpec as P

NEU = 8192
NY = 4
NZ = 8
ROWS = 640
CHUNK = 128
SUB = 80
WIDE = 1024
LOG2E = 1.4426950408889634
QSCALE = LOG2E * 0.125
LOW = -1e30
MESH = pl.DeviceIdType.MESH
F32 = jnp.float32
BF16 = jnp.bfloat16


def rms(wide, gain):
    scale = lax.rsqrt(jnp.mean(wide * wide, axis=-1, keepdims=True) + 1e-05)
    return wide * scale * gain


def nt_dot(a, b):
    return lax.dot_general(a, b, (((1,), (1,)), ((), ())), preferred_element_type=F32)


def layer_kernel(
    stream,
    gain_attn,
    gain_mlp,
    gain_read,
    wq,
    wk,
    wv,
    wo_own,
    wu_own,
    wd_own,
    out,
    xbuf,
    kvbuf,
    mirror,
    vaug,
    qrx,
    qpad,
    acc,
    best,
    otx,
    orx,
    stx,
    srx,
    att,
    slices,
    wo,
    wu,
    wd,
    rbuf,
    x_send,
    x_recv,
    kv_send,
    kv_recv,
    m_send,
    m_recv,
    q_send,
    q_recv,
    o_send,
    o_recv,
    s_send,
    s_recv,
    a_send,
    a_recv,
    w_local,
    w_send,
    w_recv,
    r_send,
    r_recv,
    l_sem,
):
    seq = lax.axis_index("seq")
    mp = lax.axis_index("mp")
    xh = seq % 2
    z = (seq // 2) % NZ
    y = seq // (2 * NZ)
    xl = mp // 2
    core = mp % 2
    x = 2 * xh + xl

    def at(y_, z_, xh_, mp_):
        return ((y_ * NZ + z_) * 2 + xh_, mp_)

    def along_x(step):
        x_ = (x + step) % 4
        return at(y, z, x_ // 2, (x_ % 2) * 2 + core)

    sibling = at(y, z, xh, xl * 2 + 1 - core)
    across = at(y, z, 1 - xh, (1 - xl) * 2 + core)
    beside = at(y, z, xh, (1 - xl) * 2 + core)
    z_up = at(y, (z + 1) % NZ, xh, mp)
    z_down = at(y, (z + NZ - 1) % NZ, xh, mp)
    mirrored = at(NY - 1 - y, z, xh, mp)

    def remote(src, dst, send, recv, device):
        return pltpu.make_async_remote_copy(
            src_ref=src,
            dst_ref=dst,
            send_sem=send,
            recv_sem=recv,
            device_id=device,
            device_id_type=MESH,
        )

    mine = 4 * xh + mp

    def group_member(step):
        e = (mine + step) % 8
        return e, at(y, z, e // 4, e % 4)

    barrier = pltpu.get_barrier_semaphore()
    for device in (
        [z_up, z_down]
        + [at((y + k) % NY, z, xh, mp) for k in range(1, NY)]
        + [group_member(k)[1] for k in range(1, 8)]
    ):
        pl.semaphore_signal(barrier, inc=1, device_id=device, device_id_type=MESH)
    pl.semaphore_wait(barrier, 12)

    half = ROWS // 4
    own_rows = pl.multiple_of(xh * (ROWS // 2), 16)
    other_rows = pl.multiple_of((1 - xh) * (ROWS // 2), 16)
    my_half = pl.multiple_of(core * half, 16)
    x_cross = remote(
        stream.at[pl.ds(my_half, half)],
        xbuf.at[pl.ds(own_rows + my_half, half)],
        x_send.at[0],
        x_recv.at[0],
        across,
    )
    x_cross.start()
    own = pltpu.make_async_copy(stream, xbuf.at[pl.ds(own_rows, ROWS // 2)], l_sem.at[0])
    own.start()

    weights = ((wo_own, wo), (wu_own, wu), (wd_own, wd))
    w_copies = []
    for i, (src, dst) in enumerate(weights):
        rows = src.shape[0]
        local = pltpu.make_async_copy(src, dst.at[mp], w_local.at[i])
        local.start()
        w_copies.append(local)
        for j, step in enumerate((1, 3)):
            part = pl.ds(j * (rows // 2), rows // 2)
            remote(
                src.at[part], dst.at[mp, part], w_send.at[i, j], w_recv.at[i, j], along_x(step)
            ).start()

    acc[...] = jnp.zeros_like(acc)
    best[...] = jnp.full_like(best, LOW)

    other_half = xbuf.at[pl.ds(other_rows + my_half, half)]
    x_forward = remote(other_half, other_half, x_send.at[1], x_recv.at[1], sibling)
    remote(other_half, other_half, x_send.at[0], x_recv.at[0], across).wait_recv()
    x_forward.start()
    own.wait()
    for i, (src, dst) in enumerate(weights):
        remote(src, dst.at[mp], w_send.at[i, 2], w_recv.at[i, 2], sibling).start()
    rest_half = xbuf.at[pl.ds(other_rows + (half - my_half), half)]
    remote(rest_half, rest_half, x_send.at[1], x_recv.at[1], sibling).wait_recv()

    lane = lax.broadcasted_iota(jnp.int32, (CHUNK, 128), 1)
    first = lane < 64
    columns = pl.ds(pl.multiple_of(xh * 128, 128), 128)
    for r in range(ROWS // CHUNK):
        rows = pl.ds(r * CHUNK, CHUNK)
        normed = rms(xbuf[rows].astype(F32), gain_attn[...]).astype(BF16)
        query = jnp.dot(normed, wq[:, columns], preferred_element_type=F32) * QSCALE
        qrx[y, rows] = query.astype(BF16)
        key = jnp.dot(normed, wk[:, columns], preferred_element_type=F32).T.astype(BF16)
        value = jnp.dot(normed, wv[:, columns], preferred_element_type=F32).T.astype(BF16)
        kvbuf[0, z, 0:64, rows] = key[0:64]
        kvbuf[0, z, 64:128, rows] = value[0:64]
        mirror[0:64, rows] = key[64:128]
        mirror[64:128, rows] = value[64:128]

    def kv_copy(h, slot, direction, d):
        block = kvbuf.at[h, slot]
        device = z_up if direction == 0 else z_down
        return remote(block, block, kv_send.at[h, direction, d], kv_recv.at[h, slot], device)

    m_copy = remote(mirror, kvbuf.at[1, z], m_send, m_recv, mirrored)
    m_copy.start()
    kv_copy(0, z, 0, 0).start()
    kv_copy(0, z, 1, 0).start()
    q_copies = []
    for k in range(1, NY):
        q_copy = remote(
            qrx.at[y], qrx.at[y], q_send.at[k - 1], q_recv.at[y], at((y + k) % NY, z, xh, mp)
        )
        q_copy.start()
        q_copies.append(q_copy)

    def unpack(s):
        for r in range(ROWS // CHUNK):
            rows = pl.ds(r * CHUNK, CHUNK)
            packed = qrx[s, rows].astype(F32)
            qpad[0, s, rows] = jnp.where(first, packed, 0.0).astype(BF16)
            qpad[1, s, rows] = jnp.where(first, pltpu.roll(packed, 64, 1), 0.0).astype(BF16)

    key_row = lax.broadcasted_iota(jnp.int32, (128, ROWS), 0)

    def prepare(h, slot):
        block = kvbuf[h, slot].astype(F32)
        vaug[...] = jnp.where(key_row < 64, 1.0, block).astype(BF16)

    def update(h, slot, s, r, keys, masked):
        rows = pl.ds(r * CHUNK, CHUNK)
        scores = jnp.dot(qpad[h, s, rows], kvbuf[h, slot, :, 0:keys], preferred_element_type=F32)
        if masked:
            query_at = lax.broadcasted_iota(jnp.int32, (CHUNK, keys), 0) + r * CHUNK
            key_at = lax.broadcasted_iota(jnp.int32, (CHUNK, keys), 1)
            scores = jnp.where(key_at <= query_at, scores, LOW)
        before = best[h, s, rows]
        fresh = jnp.maximum(before, jnp.max(scores, axis=1, keepdims=True))
        probs = jnp.exp2(scores - jnp.concatenate([fresh] * (keys // 128), axis=1)).astype(BF16)
        decay = jnp.exp2(before - fresh)
        acc[h, s, rows] = acc[h, s, rows] * decay + nt_dot(probs, vaug[:, 0:keys])
        best[h, s, rows] = fresh

    def diagonal(h, s):
        prepare(h, z)
        for r in range(ROWS // CHUNK):
            update(h, z, s, r, (r + 1) * CHUNK, True)

    def visit(h, slot, start):
        prepare(h, slot)

        def one(s, carry):
            for r in range(ROWS // CHUNK):
                update(h, slot, s, r, ROWS, False)
            return carry

        lax.fori_loop(start, NY, one, 0)

    def row_of(h):
        return y + h * (NY - 1 - 2 * y)

    unpack(y)
    diagonal(0, y)
    m_copy.wait_recv()
    kv_copy(1, z, 0, 0).start()
    kv_copy(1, z, 1, 0).start()
    for k in range(1, NY):
        s = (y + k) % NY
        remote(qrx.at[s], qrx.at[s], q_send.at[k - 1], q_recv.at[s], z_up).wait_recv()
        unpack(s)
    diagonal(1, NY - 1 - y)

    def own_visits(h, carry):
        visit(h, z, row_of(h) + 1)
        return carry

    lax.fori_loop(0, 2, own_visits, 0)

    def ring_step(u, carry):
        d = u // 2 + 1
        h = u % 2
        left = (z + NZ - d) % NZ
        right = (z + d) % NZ
        kv_copy(h, left, 0, 0).wait_recv()

        @pl.when((d < 3) | (h == 0))
        def _():
            kv_copy(h, left, 0, d).start()

        kv_copy(h, right, 1, 0).wait_recv()

        @pl.when((d < 3) | (h == 1))
        def _():
            kv_copy(h, right, 1, d).start()

        row = row_of(h)

        def side(k, carry):
            slot = left + k * (right - left)
            visit(h, slot, row + jnp.where(slot > z, 1, 0))
            return carry

        lax.fori_loop(0, 2, side, 0)
        return carry

    lax.fori_loop(0, 6, ring_step, 0)

    far = (z + NZ // 2) % NZ

    def last_step(h, carry):
        kv_copy(h, far, 0, 0).wait_recv()
        visit(h, far, row_of(h) + jnp.where(far > z, 1, 0))
        return carry

    lax.fori_loop(0, 2, last_step, 0)

    theirs = (1 - xl) * 2 + core
    for i, (src, dst) in enumerate(weights):
        rows = src.shape[0]
        for j, step in enumerate((1, 3)):
            part = pl.ds(j * (rows // 2), rows // 2)
            block = dst.at[theirs, part]
            remote(block, block, w_send.at[i, j], w_recv.at[i, j], sibling).wait_recv()
        remote(
            dst.at[theirs], dst.at[theirs], w_send.at[i, 3], w_recv.at[i, 3], sibling
        ).start()

    def partial(s, values, stats):
        for r in range(ROWS // CHUNK):
            rows = pl.ds(r * CHUNK, CHUNK)
            a0 = acc[0, s, rows]
            a1 = acc[1, s, rows]
            total = jnp.where(first, a0, pltpu.roll(a1, 64, 1))
            numer = jnp.where(first, pltpu.roll(a0, 64, 1), a1)
            some = total > 0.0
            safe = jnp.where(some, total, 1.0)
            values[rows] = (numer / safe).astype(BF16)
            high = jnp.where(first, best[0, s, rows], best[1, s, rows])
            lse = jnp.where(some, high + jnp.log(safe) * LOG2E, LOW).T
            stats[0:8, rows] = lse[0:8]
            stats[8:16, rows] = lse[64:72]

    o_copies = []
    for k in range(1, NY):
        s = (y + k) % NY
        partial(s, otx.at[k - 1], stx.at[k - 1])
        device = at(s, z, xh, mp)
        for copy in (
            remote(otx.at[k - 1], orx.at[y], o_send.at[k - 1], o_recv.at[y], device),
            remote(stx.at[k - 1], srx.at[y], s_send.at[k - 1], s_recv.at[y], device),
        ):
            copy.start()
            o_copies.append(copy)
    partial(y, orx.at[y], srx.at[y])
    for k in range(1, NY):
        s = (y + k) % NY
        remote(orx.at[s], orx.at[s], o_send.at[k - 1], o_recv.at[s], z_up).wait_recv()
        remote(srx.at[s], srx.at[s], s_send.at[k - 1], s_recv.at[s], z_up).wait_recv()
    for r in range(ROWS // CHUNK):
        rows = pl.ds(r * CHUNK, CHUNK)
        lses = []
        for s in range(NY):
            pair = [
                jnp.broadcast_to(srx[s, 8 * h : 8 * h + 1, rows], (64, CHUNK)) for h in range(2)
            ]
            lses.append(jnp.concatenate(pair, axis=0).T)
        top = jnp.maximum(jnp.maximum(lses[0], lses[1]), jnp.maximum(lses[2], lses[3]))
        numer = jnp.zeros((CHUNK, 128), F32)
        denom = jnp.zeros((CHUNK, 128), F32)
        for s in range(NY):
            weight = jnp.exp2(lses[s] - top)
            denom = denom + weight
            numer = numer + weight * orx[s, rows].astype(F32)
        att[rows] = (numer / denom).astype(BF16)

    column = 2 * mp + xh
    a_copies = []
    for k in range(1, 8):
        e, device = group_member(k)
        src = att.at[pl.ds(pl.multiple_of(e * SUB, 16), SUB)]
        copy = remote(src, slices.at[column], a_send.at[k - 1], a_recv.at[column], device)
        copy.start()
        a_copies.append(copy)
    slices[column] = att[pl.ds(pl.multiple_of(mine * SUB, 16), SUB)]
    for k in range(1, 8):
        e = (mine + k) % 8
        source = 2 * (e % 4) + e // 4
        remote(
            slices.at[source], slices.at[source], a_send.at[k - 1], a_recv.at[source], sibling
        ).wait_recv()
    for i, (src, dst) in enumerate(weights):
        w_copies[i].wait()
        near = dst.at[xl * 2 + 1 - core]
        remote(src, near, w_send.at[i, 2], w_recv.at[i, 2], sibling).wait_recv()
        away = dst.at[(1 - xl) * 2 + 1 - core]
        remote(away, away, w_send.at[i, 3], w_recv.at[i, 3], sibling).wait_recv()

    total = stream[pl.ds(pl.multiple_of(mp * SUB, 16), SUB)].astype(F32)
    for m in range(4):
        pair = jnp.concatenate([slices[2 * m], slices[2 * m + 1]], axis=1)
        total = total + jnp.dot(pair, wo[m], preferred_element_type=F32)
    resid = total.astype(BF16).astype(F32)
    mlp_in = rms(resid, gain_mlp[...]).astype(BF16)
    outcome = resid
    for m in range(4):
        hidden = jnp.dot(mlp_in, wu[m], preferred_element_type=F32)
        hidden = jax.nn.gelu(hidden, approximate=True).astype(BF16)
        outcome = outcome + jnp.dot(hidden, wd[m], preferred_element_type=F32)
    rbuf[mp] = rms(outcome, gain_read[...]).astype(BF16)

    def r_copy(slot, i, device):
        return remote(rbuf.at[slot], rbuf.at[slot], r_send.at[i], r_recv.at[i], device)

    r_copy(mp, 0, beside).start()
    r_copy(mp, 1, sibling).start()
    r_copy(theirs, 0, beside).wait_recv()
    r_copy(theirs, 2, sibling).start()
    r_copy(xl * 2 + 1 - core, 1, sibling).wait_recv()
    r_copy((1 - xl) * 2 + 1 - core, 2, sibling).wait_recv()
    for m in range(4):
        out[m * SUB : (m + 1) * SUB] = rbuf[m]

    x_cross.wait_send()
    x_forward.wait_send()
    m_copy.wait_send()
    for copy in q_copies + o_copies + a_copies:
        copy.wait_send()
    for d in range(4):
        for h in range(2):
            for direction in range(2):
                if d < 3 or h == direction:
                    kv_copy(h, z, direction, d).wait_send()
    for i, (src, dst) in enumerate(weights):
        rows = src.shape[0]
        for j in range(2):
            part = pl.ds(j * (rows // 2), rows // 2)
            remote(
                src.at[part], dst.at[mp, part], w_send.at[i, j], w_recv.at[i, j], sibling
            ).wait_send()
        remote(src, dst.at[mp], w_send.at[i, 2], w_recv.at[i, 2], sibling).wait_send()
        remote(
            dst.at[theirs], dst.at[theirs], w_send.at[i, 3], w_recv.at[i, 3], sibling
        ).wait_send()
    r_copy(mp, 0, beside).wait_send()
    r_copy(mp, 1, sibling).wait_send()
    r_copy(theirs, 2, sibling).wait_send()


def read_inputs(stream, gains, wq, wk, wv, wo, wu, wd):
    vmem = pl.BlockSpec(memory_space=pltpu.VMEM)
    hbm = pl.BlockSpec(memory_space=pl.ANY)
    dma = pltpu.SemaphoreType.DMA
    return pl.pallas_call(
        layer_kernel,
        out_shape=jax.ShapeDtypeStruct(stream.shape, BF16),
        in_specs=[vmem] * 7 + [hbm] * 3,
        out_specs=vmem,
        scratch_shapes=[
            pltpu.VMEM((ROWS, WIDE), BF16),
            pltpu.VMEM((2, NZ, 128, ROWS), BF16),
            pltpu.VMEM((128, ROWS), BF16),
            pltpu.VMEM((128, ROWS), BF16),
            pltpu.VMEM((NY, ROWS, 128), BF16),
            pltpu.VMEM((2, NY, ROWS, 128), BF16),
            pltpu.VMEM((2, NY, ROWS, 128), F32),
            pltpu.VMEM((2, NY, ROWS, 128), F32),
            pltpu.VMEM((NY - 1, ROWS, 128), BF16),
            pltpu.VMEM((NY, ROWS, 128), BF16),
            pltpu.VMEM((NY - 1, 16, ROWS), F32),
            pltpu.VMEM((NY, 16, ROWS), F32),
            pltpu.VMEM((ROWS, 128), BF16),
            pltpu.VMEM((8, SUB, 128), BF16),
            pltpu.VMEM((4,) + wo.shape, BF16),
            pltpu.VMEM((4,) + wu.shape, BF16),
            pltpu.VMEM((4,) + wd.shape, BF16),
            pltpu.VMEM((4, SUB, WIDE), BF16),
            dma((2,)),
            dma((2,)),
            dma((2, 2, 4)),
            dma((2, NZ)),
            dma,
            dma,
            dma((NY - 1,)),
            dma((NY,)),
            dma((NY - 1,)),
            dma((NY,)),
            dma((NY - 1,)),
            dma((NY,)),
            dma((7,)),
            dma((8,)),
            dma((3,)),
            dma((3, 4)),
            dma((3, 4)),
            dma((3,)),
            dma((3,)),
            dma((1,)),
        ],
        compiler_params=pltpu.CompilerParams(
            collective_id=0, has_side_effects=True, vmem_limit_bytes=60 * 1024 * 1024
        ),
    )(stream, *gains, wq, wk, wv, wo, wu, wd)


def per_device(
    stream,
    gain_attn,
    gain_mlp,
    gain_read,
    query_weight,
    key_weight,
    value_weight,
    out_weight,
    up_weight,
    down_weight,
    read_weight,
    read_bias,
    spike_counts,
):
    gains = [gain.reshape(1, WIDE) for gain in (gain_attn, gain_mlp, gain_read)]
    read_in = read_inputs(
        stream, gains, query_weight, key_weight, value_weight, out_weight, up_weight, down_weight
    )
    rate_full = jnp.dot(read_in, read_weight, preferred_element_type=F32) + read_bias
    loss_part = jnp.sum(jnp.exp(rate_full) - spike_counts.astype(F32) * rate_full, axis=-1)
    poisson_loss = lax.psum(loss_part, "mp") / NEU
    return (rate_full.astype(BF16), poisson_loss)


def solution(mesh):
    in_specs = (
        P("seq", None),
        P(),
        P(),
        P(),
        P(None, "mp"),
        P(None, "mp"),
        P(None, "mp"),
        P("mp", None),
        P(None, "mp"),
        P("mp", None),
        P(None, "mp"),
        P("mp"),
        P("seq", "mp"),
    )
    out_specs = (P("seq", "mp"), P("seq"))
    return jax.shard_map(
        per_device, mesh=mesh, in_specs=in_specs, out_specs=out_specs, check_vma=False
    )
```

time: 777 us -> 137 us (0.18)
  waiting for transfers between devices: 525 us -> 0 us
  Pallas kernels: 0 us -> 124 us
  loops' own time: 81.2 us -> 0 us
  local copies, waits for them, and re-layouts: 65.9 us -> 0.01 us
  other arithmetic: 47.4 us -> 0.58 us
  matrix products: 31.5 us -> 5.31 us
  between operations: 14 us -> 0.68 us
    all_gather x2 -> x0, waiting for transfers between devices: 311 us -> none  [the longest x1 161 us: per_device(): keys_piece = lax.all_gather(keys_flat, 'seq', axis=0, tiled=True)]
    psum x2 -> x0, waiting for transfers between devices: 215 us -> none  [the longest x1 170 us: per_device(): lax.psum(attn_part.astype(jnp.bfloat16), 'mp').astype(jnp.float32)]
    pallas_call x0 -> x1, Pallas kernels: none -> 124 us  [read_inputs(): pl.pallas_call(layer_kernel, out_shape=jax.ShapeDtypeStruct(stream.shape,...]
    another operation x41 -> x0, loops' own time: 81.2 us -> none  [the longest x1 79.8 us: per_device(): lax.scan(one_block, state, jnp.arange(block_count, dtype=jnp.int32))]
    dynamic_slice x50 -> x0, local copies, waits for them, and re-layouts: 36.9 us -> none  [the longest x40 23.5 us: per_device(): lax.scan(one_block, state, jnp.arange(block_count, dtype=jnp.int32))]
    reduce_min x40 -> x0, other arithmetic: 29.6 us -> none  [one_block(): jnp.min(block_pos) > query_last]
    unnamed x20 -> x4, local copies, waits for them, and re-layouts: 28.5 us -> 0.01 us
    dot_general x26 -> x1, matrix products: 31.5 us -> 5.31 us  [per_device(): jnp.dot(read_in, read_weight, preferred_element_type=F32) + read_bias]
  transfers between devices with their start and end apart: 4 -> 0, of which waited for: 4 -> 0; matrix products, arithmetic and copies ran while one was open for 2% -> 0% of each run, Pallas kernels for 0% -> 0%
where the time goes in v1:
time: 137 us; the launch traced here: 135 us
  Pallas kernels  124 us (91%)
  matrix products  5.31 us (4%)
  blocking collectives  5.09 us (4%)
    pallas_call x1, Pallas kernels, read_inputs(): pl.pallas_call(layer_kernel, out_shape=jax.ShapeDtypeStruct(stream.shape,...  124 us
    dot_general x1, matrix products, per_device(): jnp.dot(read_in, read_weight, preferred_element_type=F32) + read_bias  5.31 us
    psum x1, blocking collectives, per_device(): poisson_loss = lax.psum(loss_part, 'mp') / NEU  5.09 us

profile of v1, /device:TPU:225, one launch (start us, length us, event | category | flops | bytes accessed | tf_op | source)
XLA Modules:
  0.0 135.2 jit_solution(4859515296204628190)
XLA Ops:
  0.6 0.0 copy-start
  0.6 0.0 copy-start.1
  0.7 123.5 %shard_map.140 = bf16[320,1024]{1,0:T(8,128)(2,1)} custom-call(bf16[320,1024]{1,0:T(8,128)(2,1)} %stream.1, f32[1,1024]{1,0:T(1,128)} %bitcast.5, f32[1,1024]{1,0:T(1,128)} %bitcast.6, f32[1,1024]{1,0:T(1,128)} %bitcast.7, bf16[1024,256]{1,0:T(8,128)(2,1)} %wq.1, bf16[1024,256]{1,0:T(8,128)(2,1)} %wk.1, bf16[1024,256]{1,0:T(8,128)(2,1)} %wv.1, ...), custom_call_target="tpu_custom_call" | custom-call | tf_op jit(solution)/shard_map/pallas_call | solution.py:440
  124.2 0.0 copy-done
  124.2 0.0 copy-done.1
  124.2 5.3 %subtract_reduce_fusion = (f32[320]{0:T(512)S(1)}, bf16[320,2048]{1,0:T(8,128)(2,1)}) fusion(s32[320,2048]{1,0:T(8,128)S(1)} %copy-done, f32[2048]{0:T(1024)S(1)} %copy-done.1, bf16[320,1024]{1,0:T(8,128)(2,1)} %shard_map.140, bf16[1024,2048]{1,0:T(8,128)(2,1)} %param.23), kind=kOutput, calls=%fused_computation.1 | convolution fusion | flops 1346109184 | bytes 8791296 | tf_op jit(solution)/shard_map/dot_general | solution.py:510
  129.5 5.1 %psum.7 = f32[320]{0:T(512)S(1)} all-reduce(f32[320]{0:T(512)S(1)} %get-tuple-element.2), channel_id=1, replica_groups=mesh['seq'=64,'mp'=4] {'mp'}, use_global_device_ids=true, to_apply=%region_1.0 | all-reduce | flops 320 | bytes 2560 | tf_op jit(solution)/shard_map/psum | solution.py:512
  134.6 0.6 broadcast_multiply_fusion
Async XLA Ops:
  0.6 123.5 %copy-start = (s32[320,2048]{1,0:T(8,128)S(1)}, s32[320,2048]{1,0:T(8,128)}, u32[]{:S(2)}) copy-start(s32[320,2048]{1,0:T(8,128)} %param.25) | copy-start | bytes 7864324
  0.6 123.5 %copy-start.1 = (f32[2048]{0:T(1024)S(1)}, f32[2048]{0:T(1024)}, u32[]{:S(2)}) copy-start(f32[2048]{0:T(1024)} %param.24) | copy-start | bytes 24580

commit v2 on v1

--- a/solution.py
+++ b/solution.py
@@ -12,6 +12,7 @@
 CHUNK = 128
 SUB = 80
 WIDE = 1024
+TILE = 512
 LOG2E = 1.4426950408889634
 QSCALE = LOG2E * 0.125
 LOW = -1e30
@@ -30,17 +31,29 @@
 
 
 def layer_kernel(
-    stream,
     gain_attn,
     gain_mlp,
     gain_read,
+    bias,
+    stream,
+    wq_own,
+    wk_own,
+    wv_own,
+    wo_own,
+    wu_own,
+    wd_own,
+    read_own,
+    spikes_own,
+    out,
+    loss,
     wq,
     wk,
     wv,
-    wo_own,
-    wu_own,
-    wd_own,
-    out,
+    wread,
+    spikes,
+    read_in,
+    terms,
+    lossbuf,
     xbuf,
     kvbuf,
     mirror,
@@ -78,6 +91,8 @@
     w_recv,
     r_send,
     r_recv,
+    t_send,
+    t_recv,
     l_sem,
 ):
     seq = lax.axis_index("seq")
@@ -119,6 +134,16 @@
         e = (mine + step) % 8
         return e, at(y, z, e // 4, e % 4)
 
+    columns = pl.ds(pl.multiple_of(xh * 128, 128), 128)
+    early = []
+    for i, (src, dst) in enumerate(((wq_own, wq), (wk_own, wk), (wv_own, wv))):
+        copy = pltpu.make_async_copy(src.at[:, columns], dst, l_sem.at[1 + i])
+        copy.start()
+        early.append(copy)
+    own_rows = pl.multiple_of(xh * (ROWS // 2), 16)
+    own = pltpu.make_async_copy(stream, xbuf.at[pl.ds(own_rows, ROWS // 2)], l_sem.at[0])
+    own.start()
+
     barrier = pltpu.get_barrier_semaphore()
     for device in (
         [z_up, z_down]
@@ -129,7 +154,6 @@
     pl.semaphore_wait(barrier, 12)
 
     half = ROWS // 4
-    own_rows = pl.multiple_of(xh * (ROWS // 2), 16)
     other_rows = pl.multiple_of((1 - xh) * (ROWS // 2), 16)
     my_half = pl.multiple_of(core * half, 16)
     x_cross = remote(
@@ -140,8 +164,6 @@
         across,
     )
     x_cross.start()
-    own = pltpu.make_async_copy(stream, xbuf.at[pl.ds(own_rows, ROWS // 2)], l_sem.at[0])
-    own.start()
 
     weights = ((wo_own, wo), (wu_own, wu), (wd_own, wd))
     w_copies = []
@@ -171,14 +193,15 @@
 
     lane = lax.broadcasted_iota(jnp.int32, (CHUNK, 128), 1)
     first = lane < 64
-    columns = pl.ds(pl.multiple_of(xh * 128, 128), 128)
+    for copy in early:
+        copy.wait()
     for r in range(ROWS // CHUNK):
         rows = pl.ds(r * CHUNK, CHUNK)
         normed = rms(xbuf[rows].astype(F32), gain_attn[...]).astype(BF16)
-        query = jnp.dot(normed, wq[:, columns], preferred_element_type=F32) * QSCALE
+        query = jnp.dot(normed, wq[...], preferred_element_type=F32) * QSCALE
         qrx[y, rows] = query.astype(BF16)
-        key = jnp.dot(normed, wk[:, columns], preferred_element_type=F32).T.astype(BF16)
-        value = jnp.dot(normed, wv[:, columns], preferred_element_type=F32).T.astype(BF16)
+        key = jnp.dot(normed, wk[...], preferred_element_type=F32).T.astype(BF16)
+        value = jnp.dot(normed, wv[...], preferred_element_type=F32).T.astype(BF16)
         kvbuf[0, z, 0:64, rows] = key[0:64]
         kvbuf[0, z, 64:128, rows] = value[0:64]
         mirror[0:64, rows] = key[64:128]
@@ -200,6 +223,13 @@
         )
         q_copy.start()
         q_copies.append(q_copy)
+
+    late = [
+        pltpu.make_async_copy(read_own, wread, l_sem.at[4]),
+        pltpu.make_async_copy(spikes_own, spikes, l_sem.at[5]),
+    ]
+    for copy in late:
+        copy.start()
 
     def unpack(s):
         for r in range(ROWS // CHUNK):
@@ -382,7 +412,7 @@
         away = dst.at[(1 - xl) * 2 + 1 - core]
         remote(away, away, w_send.at[i, 3], w_recv.at[i, 3], sibling).wait_recv()
 
-    total = stream[pl.ds(pl.multiple_of(mp * SUB, 16), SUB)].astype(F32)
+    total = xbuf[pl.ds(pl.multiple_of(own_rows + mp * SUB, 16), SUB)].astype(F32)
     for m in range(4):
         pair = jnp.concatenate([slices[2 * m], slices[2 * m + 1]], axis=1)
         total = total + jnp.dot(pair, wo[m], preferred_element_type=F32)
@@ -405,12 +435,45 @@
     r_copy(xl * 2 + 1 - core, 1, sibling).wait_recv()
     r_copy((1 - xl) * 2 + 1 - core, 2, sibling).wait_recv()
     for m in range(4):
-        out[m * SUB : (m + 1) * SUB] = rbuf[m]
+        read_in[m * SUB : (m + 1) * SUB] = rbuf[m]
+    for copy in late:
+        copy.wait()
+
+    terms[...] = jnp.zeros_like(terms)
+
+    def readout(t, carry):
+        tile = pl.ds(pl.multiple_of(t * TILE, TILE), TILE)
+        rate = jnp.dot(read_in[...], wread[:, tile], preferred_element_type=F32) + bias[:, tile]
+        out[:, tile] = rate.astype(BF16)
+        term = jnp.exp(rate) - spikes[:, tile].astype(F32) * rate
+        folded = term[:, 0:128]
+        for i in range(1, TILE // 128):
+            folded = folded + term[:, i * 128 : (i + 1) * 128]
+        terms[0 : 4 * SUB] = terms[0 : 4 * SUB] + folded
+        return carry
+
+    lax.fori_loop(0, wread.shape[1] // TILE, readout, 0)
+    for r in range(3):
+        rows = pl.ds(r * 128, 128)
+        part = jnp.sum(terms[rows].T, axis=0, keepdims=True)
+        lossbuf[mp, :, rows] = jnp.broadcast_to(part, (8, 128))
+    t_copies = []
+    for k in range(1, 4):
+        copy = remote(
+            lossbuf.at[mp], lossbuf.at[mp], t_send.at[k - 1], t_recv.at[mp], at(y, z, xh, (mp + k) % 4)
+        )
+        copy.start()
+        t_copies.append(copy)
+    for k in range(1, 4):
+        m = (mp + k) % 4
+        remote(lossbuf.at[m], lossbuf.at[m], t_send.at[k - 1], t_recv.at[m], sibling).wait_recv()
+    summed = (lossbuf[0] + lossbuf[1]) + (lossbuf[2] + lossbuf[3])
+    loss[...] = summed[0:1, 0 : 4 * SUB] / NEU
 
     x_cross.wait_send()
     x_forward.wait_send()
     m_copy.wait_send()
-    for copy in q_copies + o_copies + a_copies:
+    for copy in q_copies + o_copies + a_copies + t_copies:
         copy.wait_send()
     for d in range(4):
         for h in range(2):
@@ -433,16 +496,27 @@
     r_copy(theirs, 2, sibling).wait_send()
 
 
-def read_inputs(stream, gains, wq, wk, wv, wo, wu, wd):
+def layer(gains, bias, stream, wq, wk, wv, wo, wu, wd, read_weight, spikes):
     vmem = pl.BlockSpec(memory_space=pltpu.VMEM)
     hbm = pl.BlockSpec(memory_space=pl.ANY)
     dma = pltpu.SemaphoreType.DMA
     return pl.pallas_call(
         layer_kernel,
-        out_shape=jax.ShapeDtypeStruct(stream.shape, BF16),
-        in_specs=[vmem] * 7 + [hbm] * 3,
-        out_specs=vmem,
+        out_shape=(
+            jax.ShapeDtypeStruct(spikes.shape, BF16),
+            jax.ShapeDtypeStruct((1, spikes.shape[0]), F32),
+        ),
+        in_specs=[vmem] * 4 + [hbm] * 9,
+        out_specs=(vmem, vmem),
         scratch_shapes=[
+            pltpu.VMEM((WIDE, 128), BF16),
+            pltpu.VMEM((WIDE, 128), BF16),
+            pltpu.VMEM((WIDE, 128), BF16),
+            pltpu.VMEM(read_weight.shape, BF16),
+            pltpu.VMEM(spikes.shape, jnp.int32),
+            pltpu.VMEM(stream.shape, BF16),
+            pltpu.VMEM((384, 128), F32),
+            pltpu.VMEM((4, 8, 384), F32),
             pltpu.VMEM((ROWS, WIDE), BF16),
             pltpu.VMEM((2, NZ, 128, ROWS), BF16),
             pltpu.VMEM((128, ROWS), BF16),
@@ -480,12 +554,14 @@
             dma((3, 4)),
             dma((3,)),
             dma((3,)),
-            dma((1,)),
+            dma((3,)),
+            dma((4,)),
+            dma((6,)),
         ],
         compiler_params=pltpu.CompilerParams(
             collective_id=0, has_side_effects=True, vmem_limit_bytes=60 * 1024 * 1024
         ),
-    )(stream, *gains, wq, wk, wv, wo, wu, wd)
+    )(*gains, bias, stream, wq, wk, wv, wo, wu, wd, read_weight, spikes)
 
 
 def per_device(
@@ -504,13 +580,20 @@
     spike_counts,
 ):
     gains = [gain.reshape(1, WIDE) for gain in (gain_attn, gain_mlp, gain_read)]
-    read_in = read_inputs(
-        stream, gains, query_weight, key_weight, value_weight, out_weight, up_weight, down_weight
+    log_rate, poisson_loss = layer(
+        gains,
+        read_bias.reshape(1, -1),
+        stream,
+        query_weight,
+        key_weight,
+        value_weight,
+        out_weight,
+        up_weight,
+        down_weight,
+        read_weight,
+        spike_counts,
     )
-    rate_full = jnp.dot(read_in, read_weight, preferred_element_type=F32) + read_bias
-    loss_part = jnp.sum(jnp.exp(rate_full) - spike_counts.astype(F32) * rate_full, axis=-1)
-    poisson_loss = lax.psum(loss_part, "mp") / NEU
-    return (rate_full.astype(BF16), poisson_loss)
+    return (log_rate, poisson_loss.reshape(-1))
 
 
 def solution(mesh):

time: 137 us -> 133 us (0.971)
  matrix products: 5.31 us -> 0 us
  blocking collectives: 5.09 us -> 0 us
  Pallas kernels: 124 us -> 128 us
  local copies, waits for them, and re-layouts: 0.01 us -> 2.52 us
    dot_general x1 -> x0, matrix products: 5.31 us -> none  [per_device(): jnp.dot(read_in, read_weight, preferred_element_type=F32) + read_bias]
    psum x1 -> x0, blocking collectives: 5.09 us -> none  [per_device(): poisson_loss = lax.psum(loss_part, 'mp') / NEU]
    pallas_call x1, Pallas kernels: 124 us -> 128 us  [layer(): pl.pallas_call(layer_kernel, out_shape=(jax.ShapeDtypeStruct(spikes.shape...]
    unnamed x4 -> x1, local copies, waits for them, and re-layouts: 0.01 us -> 2.52 us
where the time goes in v2:
time: 133 us
  Pallas kernels  128 us (96%)
  local copies, waits for them, and re-layouts  2.52 us (2%)
    pallas_call x1, Pallas kernels, layer(): pl.pallas_call(layer_kernel, out_shape=(jax.ShapeDtypeStruct(spikes.shape...  128 us

profile of v2, /device:TPU:225, one launch (start us, length us, event | category | flops | bytes accessed | tf_op | source)
XLA Modules:
  0.0 132.5 jit_solution(1053912289148547655)
XLA Ops:
  0.6 128.1 %shard_map.140 = (bf16[320,2048]{1,0:T(8,128)(2,1)}, f32[1,320]{1,0:T(1,128)}) custom-call(f32[1,1024]{1,0:T(1,128)} %bitcast.5, f32[1,1024]{1,0:T(1,128)} %bitcast.6, f32[1,1024]{1,0:T(1,128)} %bitcast.7, f32[1,2048]{1,0:T(1,128)} %bitcast.4, bf16[320,1024]{1,0:T(8,128)(2,1)} %stream.1, bf16[1024,256]{1,0:T(8,128)(2,1)} %wq_own.1, ...), custom_call_target="tpu_custom_call" | custom-call | tf_op jit(solution)/shard_map/pallas_call | solution.py:503
  128.8 1.2 reduce
  130.0 2.5 %copy.16 = bf16[320,2048]{1,0:T(8,128)(2,1)} copy(bf16[320,2048]{1,0:T(8,128)(2,1)} %get-tuple-element.8) | data formatting | bytes 2621440

commit v3 on v2

--- a/solution.py
+++ b/solution.py
@@ -10,6 +10,7 @@
 NZ = 8
 ROWS = 640
 CHUNK = 128
+BAND = 320
 SUB = 80
 WIDE = 1024
 TILE = 512
@@ -244,12 +245,12 @@
         block = kvbuf[h, slot].astype(F32)
         vaug[...] = jnp.where(key_row < 64, 1.0, block).astype(BF16)
 
-    def update(h, slot, s, r, keys, masked):
-        rows = pl.ds(r * CHUNK, CHUNK)
+    def update(h, slot, s, r, size, keys, masked):
+        rows = pl.ds(r * size, size)
         scores = jnp.dot(qpad[h, s, rows], kvbuf[h, slot, :, 0:keys], preferred_element_type=F32)
         if masked:
-            query_at = lax.broadcasted_iota(jnp.int32, (CHUNK, keys), 0) + r * CHUNK
-            key_at = lax.broadcasted_iota(jnp.int32, (CHUNK, keys), 1)
+            query_at = lax.broadcasted_iota(jnp.int32, (size, keys), 0) + r * size
+            key_at = lax.broadcasted_iota(jnp.int32, (size, keys), 1)
             scores = jnp.where(key_at <= query_at, scores, LOW)
         before = best[h, s, rows]
         fresh = jnp.maximum(before, jnp.max(scores, axis=1, keepdims=True))
@@ -261,14 +262,14 @@
     def diagonal(h, s):
         prepare(h, z)
         for r in range(ROWS // CHUNK):
-            update(h, z, s, r, (r + 1) * CHUNK, True)
+            update(h, z, s, r, CHUNK, (r + 1) * CHUNK, True)
 
     def visit(h, slot, start):
         prepare(h, slot)
 
         def one(s, carry):
-            for r in range(ROWS // CHUNK):
-                update(h, slot, s, r, ROWS, False)
+            for r in range(ROWS // BAND):
+                update(h, slot, s, r, BAND, ROWS, False)
             return carry
 
         lax.fori_loop(start, NY, one, 0)
@@ -430,29 +431,34 @@
 
     r_copy(mp, 0, beside).start()
     r_copy(mp, 1, sibling).start()
+    r_copy(xl * 2 + 1 - core, 1, sibling).wait_recv()
+    for copy in late:
+        copy.wait()
+    terms[...] = jnp.zeros_like(terms)
+
+    def readout(chip):
+        rows = pl.ds(pl.multiple_of(chip * (2 * SUB), 32), 2 * SUB)
+        read_in[...] = jnp.concatenate([rbuf[2 * chip], rbuf[2 * chip + 1]], axis=0)
+
+        def columns_of(t, carry):
+            tile = pl.ds(pl.multiple_of(t * TILE, TILE), TILE)
+            rate = jnp.dot(read_in[...], wread[:, tile], preferred_element_type=F32)
+            rate = rate + bias[:, tile]
+            out[rows, tile] = rate.astype(BF16)
+            term = jnp.exp(rate) - spikes[rows, tile].astype(F32) * rate
+            folded = term[:, 0:128]
+            for i in range(1, TILE // 128):
+                folded = folded + term[:, i * 128 : (i + 1) * 128]
+            terms[rows] = terms[rows] + folded
+            return carry
+
+        lax.fori_loop(0, wread.shape[1] // TILE, columns_of, 0)
+
+    readout(xl)
     r_copy(theirs, 0, beside).wait_recv()
     r_copy(theirs, 2, sibling).start()
-    r_copy(xl * 2 + 1 - core, 1, sibling).wait_recv()
     r_copy((1 - xl) * 2 + 1 - core, 2, sibling).wait_recv()
-    for m in range(4):
-        read_in[m * SUB : (m + 1) * SUB] = rbuf[m]
-    for copy in late:
-        copy.wait()
-
-    terms[...] = jnp.zeros_like(terms)
-
-    def readout(t, carry):
-        tile = pl.ds(pl.multiple_of(t * TILE, TILE), TILE)
-        rate = jnp.dot(read_in[...], wread[:, tile], preferred_element_type=F32) + bias[:, tile]
-        out[:, tile] = rate.astype(BF16)
-        term = jnp.exp(rate) - spikes[:, tile].astype(F32) * rate
-        folded = term[:, 0:128]
-        for i in range(1, TILE // 128):
-            folded = folded + term[:, i * 128 : (i + 1) * 128]
-        terms[0 : 4 * SUB] = terms[0 : 4 * SUB] + folded
-        return carry
-
-    lax.fori_loop(0, wread.shape[1] // TILE, readout, 0)
+    readout(1 - xl)
     for r in range(3):
         rows = pl.ds(r * 128, 128)
         part = jnp.sum(terms[rows].T, axis=0, keepdims=True)
@@ -514,7 +520,7 @@
             pltpu.VMEM((WIDE, 128), BF16),
             pltpu.VMEM(read_weight.shape, BF16),
             pltpu.VMEM(spikes.shape, jnp.int32),
-            pltpu.VMEM(stream.shape, BF16),
+            pltpu.VMEM((2 * SUB, WIDE), BF16),
             pltpu.VMEM((384, 128), F32),
             pltpu.VMEM((4, 8, 384), F32),
             pltpu.VMEM((ROWS, WIDE), BF16),

time: 133 us -> 110 us (0.83)
  Pallas kernels: 128 us -> 105 us
    pallas_call x1, Pallas kernels: 128 us -> 105 us  [layer(): pl.pallas_call(layer_kernel, out_shape=(jax.ShapeDtypeStruct(spikes.shape...]
where the time goes in v3:
time: 110 us
  Pallas kernels  105 us (95%)
  local copies, waits for them, and re-layouts  2.52 us (2%)
  other arithmetic  1.23 us (1%)
    pallas_call x1, Pallas kernels, layer(): pl.pallas_call(layer_kernel, out_shape=(jax.ShapeDtypeStruct(spikes.shape...  105 us
    unnamed x1, local copies, waits for them, and re-layouts  2.52 us

profile of v3, /device:TPU:225, one launch (start us, length us, event | category | flops | bytes accessed | tf_op | source)
XLA Modules:
  0.0 109.8 jit_solution(17792914777065270775)
XLA Ops:
  0.6 105.4 %shard_map.140 = (bf16[320,2048]{1,0:T(8,128)(2,1)}, f32[1,320]{1,0:T(1,128)}) custom-call(f32[1,1024]{1,0:T(1,128)} %bitcast.5, f32[1,1024]{1,0:T(1,128)} %bitcast.6, f32[1,1024]{1,0:T(1,128)} %bitcast.7, f32[1,2048]{1,0:T(1,128)} %bitcast.4, bf16[320,1024]{1,0:T(8,128)(2,1)} %stream.1, bf16[1024,256]{1,0:T(8,128)(2,1)} %wq_own.1, ...), custom_call_target="tpu_custom_call" | custom-call | tf_op jit(solution)/shard_map/pallas_call | solution.py:509
  106.1 1.2 %reduce = f32[320]{0:T(512)} reduce(f32[1,320]{1,0:T(1,128)} %get-tuple-element.5, f32[]{:T(128)} %constant), dimensions={0}, to_apply=%get-tuple-element.5.reduce_sub_computation | reduce | bytes 2564 | tf_op jit(solution)/shard_map/pallas_call | solution.py:509
  107.3 2.5 %copy.16 = bf16[320,2048]{1,0:T(8,128)(2,1)} copy(bf16[320,2048]{1,0:T(8,128)(2,1)} %get-tuple-element.8) | data formatting | bytes 2621440

commit v4 on v3

--- a/solution.py
+++ b/solution.py
@@ -10,7 +10,7 @@
 NZ = 8
 ROWS = 640
 CHUNK = 128
-BAND = 320
+BAND = 640
 SUB = 80
 WIDE = 1024
 TILE = 512
@@ -261,8 +261,8 @@
 
     def diagonal(h, s):
         prepare(h, z)
-        for r in range(ROWS // CHUNK):
-            update(h, z, s, r, CHUNK, (r + 1) * CHUNK, True)
+        update(h, z, s, 0, ROWS // 2, 3 * CHUNK, True)
+        update(h, z, s, 1, ROWS // 2, ROWS, True)
 
     def visit(h, slot, start):
         prepare(h, slot)

time: 110 us -> 107 us (0.973)
  Pallas kernels: 105 us -> 102 us
    pallas_call x1, Pallas kernels: 105 us -> 102 us  [layer(): pl.pallas_call(layer_kernel, out_shape=(jax.ShapeDtypeStruct(spikes.shape...]
where the time goes in v4:
time: 107 us
  Pallas kernels  102 us (95%)
  local copies, waits for them, and re-layouts  2.52 us (2%)
  other arithmetic  1.23 us (1%)
    pallas_call x1, Pallas kernels, layer(): pl.pallas_call(layer_kernel, out_shape=(jax.ShapeDtypeStruct(spikes.shape...  102 us
    unnamed x1, local copies, waits for them, and re-layouts  2.52 us

profile of v4, /device:TPU:225, one launch (start us, length us, event | category | flops | bytes accessed | tf_op | source)
XLA Modules:
  0.0 106.6 jit_solution(5180143830730160954)
XLA Ops:
  0.6 102.2 %shard_map.140 = (bf16[320,2048]{1,0:T(8,128)(2,1)}, f32[1,320]{1,0:T(1,128)}) custom-call(f32[1,1024]{1,0:T(1,128)} %bitcast.5, f32[1,1024]{1,0:T(1,128)} %bitcast.6, f32[1,1024]{1,0:T(1,128)} %bitcast.7, f32[1,2048]{1,0:T(1,128)} %bitcast.4, bf16[320,1024]{1,0:T(8,128)(2,1)} %stream.1, bf16[1024,256]{1,0:T(8,128)(2,1)} %wq_own.1, ...), custom_call_target="tpu_custom_call" | custom-call | tf_op jit(solution)/shard_map/pallas_call | solution.py:509
  102.8 1.2 %reduce = f32[320]{0:T(512)} reduce(f32[1,320]{1,0:T(1,128)} %get-tuple-element.5, f32[]{:T(128)} %constant), dimensions={0}, to_apply=%get-tuple-element.5.reduce_sub_computation | reduce | bytes 2564 | tf_op jit(solution)/shard_map/pallas_call | solution.py:509
  104.0 2.5 %copy.16 = bf16[320,2048]{1,0:T(8,128)(2,1)} copy(bf16[320,2048]{1,0:T(8,128)(2,1)} %get-tuple-element.8) | data formatting | bytes 2621440
